TPU v7x, 512 devices: a whole 4x8x8 slice. The times are simulated.
512 devices in a mesh: req: 128 (over y, z, core), tp: 4 (over x).
Axes of the slice: x: 4, y: 8, z: 8, core: 2. Of those that a mesh axis runs over, the one named last changes fastest.
Arguments:
- attn_out: bfloat16 [8192, 2048], P('req', 'tp'), may hold values from -6 to 6
- w_out: bfloat16 [2048, 2048], P('tp'), may hold values from -0.125 to 0.125
- residual: bfloat16 [8192, 2048], P('req', 'tp'), may hold values from -6 to 6
- routes: int32 [8192, 6], P('req'), may hold values from 0 to 127, all different within a row; in each aligned block of 64 rows (0 to 63, 64 to 127, ...) at most 6 rows name the same one
- gates: float32 [8192, 6], P('req'), may hold values from 0.05 to 1
- w_gate: bfloat16 [128, 2048, 1024], P('req', None, 'tp'), as said below
- w_up: bfloat16 [128, 2048, 1024], P('req', None, 'tp'), as said below
- w_down: bfloat16 [128, 1024, 2048], P('req', None, 'tp'), as said below
- norm_gain: float32 [2048], P('tp'), may hold values from 0.1 to 1.9
Outputs:
- normed: bfloat16 [8192, 2048], P('req', 'tp')
Inputs may be any that keep to these rules, and one draw needn't show every extreme that they name: `routes`: each row names 6 different slots. In the 64 rows of one index of req no slot is named by more than 6 rows, a bound that some block reaches. `w_gate`: slots 2 e and 2 e + 1 hold the same expert e: their weights are equal. `w_up`: slots 2 e and 2 e + 1 hold the same expert e: their weights are equal. `w_down`: slots 2 e and 2 e + 1 hold the same expert e: their weights are equal.
All inputs are finite; a program needn't handle non-finite values.
Results may differ from a plain program's by a relative error of at most 0.0056.
Values may be sent and summed in bfloat16 or wider, within the bound.
A program may use at most 64 MiB of HBM per device.

v0:
```python
import jax
import jax.numpy as jnp
from jax import lax
from jax.sharding import PartitionSpec as P


def body(attn_out, w_out, residual, routes, gates, w_gate, w_up, w_down, norm_gain):
    row_count = attn_out.shape[0]
    part_width = residual.shape[1]
    full_width = w_out.shape[1]
    route_count = routes.shape[1]
    slot_count = lax.axis_size("req")
    capacity = max(2, min(row_count, 2 * row_count * route_count // slot_count))
    tp_index = lax.axis_index("tp")
    partial_value = jnp.dot(attn_out, w_out, preferred_element_type=jnp.float32)
    own_block = lax.dynamic_slice_in_dim(partial_value, tp_index * part_width, part_width, 1)
    partial_value = lax.dynamic_update_slice_in_dim(
        partial_value, own_block + residual.astype(jnp.float32), tp_index * part_width, 1
    )
    flat_routes = routes.reshape(-1)
    one_hot = (flat_routes[:, None] == jnp.arange(slot_count, dtype=jnp.int32)[None, :]).astype(
        jnp.int32
    )
    position = jnp.sum(one_hot * (jnp.cumsum(one_hot, axis=0) - 1), axis=1)
    dest_index = flat_routes * capacity + position
    row_ids = jnp.repeat(jnp.arange(row_count, dtype=jnp.int32), route_count)
    source_row = jnp.zeros((slot_count * capacity,), jnp.int32).at[dest_index].set(row_ids)
    gate_local = w_gate[0]
    up_local = w_up[0]
    down_local = w_down[0]
    projected = lax.psum(partial_value, "tp")
    own_part = lax.dynamic_slice_in_dim(projected, tp_index * part_width, part_width, 1)
    outgoing = projected.astype(jnp.bfloat16)[source_row].reshape(slot_count, capacity, full_width)
    incoming = lax.all_to_all(outgoing, "req", split_axis=0, concat_axis=0, tiled=True)
    expert_rows = incoming.reshape(slot_count * capacity, full_width)
    gate_act = jnp.dot(expert_rows, gate_local, preferred_element_type=jnp.float32)
    up_act = jnp.dot(expert_rows, up_local, preferred_element_type=jnp.float32)
    hidden = (jax.nn.silu(gate_act) * up_act).astype(jnp.bfloat16)
    expert_out = jnp.dot(
        lax.all_gather(hidden, "tp", axis=1, tiled=True),
        down_local,
        preferred_element_type=jnp.float32,
    )
    expert_out = expert_out.astype(jnp.bfloat16).reshape(slot_count, capacity, down_local.shape[1])
    returned = lax.all_to_all(expert_out, "req", split_axis=0, concat_axis=0, tiled=True)
    picked = returned.reshape(slot_count * capacity, part_width)[dest_index]
    picked = picked.reshape(row_count, route_count, part_width).astype(jnp.float32)
    routed_sum = jnp.sum(picked * gates[:, :, None], axis=1)
    combined = own_part + routed_sum
    square_part = jnp.sum(combined * combined, axis=1)
    square_total = lax.psum(square_part, "tp")
    scale = lax.rsqrt(square_total / full_width + 1e-06)
    return (combined * scale[:, None] * norm_gain[None, :]).astype(jnp.bfloat16)


def solution(mesh):
    placed = (
        P("req", "tp"),
        P("tp", None),
        P("req", "tp"),
        P("req", None),
        P("req", None),
        P("req", None, "tp"),
        P("req", None, "tp"),
        P("req", None, "tp"),
        P("tp"),
    )
    return jax.shard_map(
        body, mesh=mesh, in_specs=placed, out_specs=P("req", "tp"), check_vma=False
    )
```

profile of v0, /device:TPU:8, one launch (start us, length us, event | category | flops | bytes accessed | tf_op | source)
XLA Modules:
  0.0 315.9 jit_solution(1539475655118343820)
XLA Ops:
  6.5 1.6 copy-done
  8.1 1.3 fusion.12
  9.4 0.9 add_dynamic-update-slice_fusion
  10.3 0.8 copy-done.2
  12.7 2.9 scatter_custom_fusion
  15.6 53.9 %all-reduce.2.cloned.1.call-done = f32[64,2048]{1,0:T(8,128)} async-done(((f32[64,2048]{1,0:T(8,128)}), f32[64,2048]{1,0:T(8,128)}) %all-reduce.2.cloned.1.call-update) | async-done | bytes 524304 | tf_op jit(solution)/shard_map/psum | solution.py:31
  69.5 1.1 convert_element_type.27
  70.6 4.3 %gather_fusion = bf16[768,2048]{1,0:T(8,128)(2,1)} fusion(bf16[64,2048]{1,0:T(8,128)(2,1)S(1)} %convert_element_type.27, s32[1024]{0:T(1024)S(1)} %pad_clamp_fusion.1), kind=kCustom, calls=%fused_computation | custom fusion | bytes 6294528 | tf_op jit(solution)/shard_map/gather | solution.py:33
  74.9 6.3 %reshape.71 = bf16[128,6,2048]{2,1,0:T(8,128)(2,1)} reshape(bf16[768,2048]{1,0:T(8,128)(2,1)} %gather_fusion) | data formatting | bytes 6291456 | tf_op jit(solution)/shard_map/reshape | solution.py:33
  81.1 111.0 %all_to_all.10 = bf16[128,6,2048]{2,1,0:T(8,128)(2,1)} all-to-all(bf16[128,6,2048]{2,1,0:T(8,128)(2,1)} %reshape.71), channel_id=1, replica_groups=mesh['req'=128,'tp'=4] {'req'}, dimensions={0} | all-to-all | bytes 6291456 | tf_op jit(solution)/shard_map/all_to_all | solution.py:34
  192.1 6.3 %reshape.72 = bf16[768,2048]{1,0:T(8,128)(2,1)} reshape(bf16[128,6,2048]{2,1,0:T(8,128)(2,1)} %all_to_all.10) | data formatting | bytes 6291456 | tf_op jit(solution)/shard_map/reshape | solution.py:35
  198.4 3.3 %fusion.3 = f32[768,256]{1,0:T(8,128)S(1)} fusion(bf16[768,2048]{1,0:T(8,128)(2,1)} %reshape.72, bf16[1,2048,256]{2,1,0:T(8,128)(2,1)} %param.14), kind=kOutput, calls=%fused_computation.8 | convolution fusion | flops 805306368 | bytes 4980736 | tf_op jit(solution)/shard_map/dot_general | solution.py:36
  201.9 1.7 fusion
  203.6 38.7 %all-gather.2.cloned.1.call-done = bf16[768,1024]{1,0:T(8,128)(2,1)} async-done(((bf16[768,256]{1,0:T(8,128)(2,1)}), bf16[768,1024]{1,0:T(8,128)(2,1)}) %all-gather.2.cloned.1.call-update) | async-done | bytes 1572880 | tf_op jit(solution)/shard_map/all_gather | solution.py:40
  242.3 2.7 convolution_convert_fusion
  245.0 1.3 reshape.73
  246.3 14.6 %all-to-all-start.1 = ((bf16[128,6,512]{2,1,0:T(8,128)(2,1)}), bf16[128,6,512]{2,1,0:T(8,128)(2,1)}, u32[]{:S(2)}, u32[]{:S(2)}) async-start(bf16[128,6,512]{2,1,0:T(8,128)(2,1)} %reshape.73), calls=%async_computation.1 | async-start | bytes 2097152 | tf_op jit(solution)/shard_map/all_to_all | solution.py:45
  261.6 30.2 %all-to-all-done.1 = bf16[128,6,512]{2,1,0:T(8,128)(2,1)} async-done(((bf16[128,6,512]{2,1,0:T(8,128)(2,1)}), bf16[128,6,512]{2,1,0:T(8,128)(2,1)}, u32[]{:S(2)}, u32[]{:S(2)}) %all-to-all-start.1) | async-done | bytes 786464 | tf_op jit(solution)/shard_map/all_to_all | solution.py:45
  291.9 1.4 reshape.74
  293.3 2.1 gather_fusion.1
  295.4 1.1 multiply_reduce_fusion
  296.6 1.0 multiply_reduce_fusion.1
  297.6 9.8 %psum.15 = f32[64]{0:T(128)S(1)} all-reduce(f32[64]{0:T(128)S(1)} %multiply_reduce_fusion.1), channel_id=1, replica_groups=mesh['req'=128,'tp'=4] {'tp'}, use_global_device_ids=true, to_apply=%region_7.8 | all-reduce | flops 64 | bytes 512 | tf_op jit(solution)/shard_map/psum | solution.py:51
  307.4 1.6 multiply_convert_fusion
  (38 shorter events, 2.5 us)
Async XLA Ops:
  6.5 1.6 copy-start
  6.5 4.6 %copy-start.3 = (s32[64,6]{0,1:T(8,128)S(1)}, s32[64,6]{0,1:T(8,128)}, u32[]{:S(2)}) copy-start(s32[64,6]{0,1:T(8,128)} %param.12) | copy-start | bytes 4612
  6.5 63.0 %all-reduce.2.cloned.1.call-start = ((), (), s32[]{:S(2)}) async-start(), calls=%async_computation.2 | async-start | bytes 1048576 | tf_op jit(solution)/shard_map/psum | solution.py:31
  10.3 0.8 copy-start.2
  11.1 231.1 %all-gather.2.cloned.1.call-start = ((), (), s32[]{:S(2)}) async-start(), calls=%async_computation.3 | async-start | bytes 1966080 | tf_op jit(solution)/shard_map/all_gather | solution.py:40
  198.4 3.3 %copy-start.1 = (bf16[768,2048]{1,0:T(8,128)(2,1)S(1)}, bf16[768,2048]{1,0:T(8,128)(2,1)}, u32[]{:S(2)}) copy-start(bf16[768,2048]{1,0:T(8,128)(2,1)} %reshape.72) | copy-start | bytes 9437188
  198.4 3.4 %copy-start.6 = (bf16[1,2048,256]{2,1,0:T(8,128)(2,1)S(1)}, bf16[1,2048,256]{2,1,0:T(8,128)(2,1)}, u32[]{:S(2)}) copy-start(bf16[1,2048,256]{2,1,0:T(8,128)(2,1)} %param.15) | copy-start | bytes 3145732
  245.0 15.9 %copy-start.4 = (f32[64,6]{0,1:T(8,128)S(1)}, f32[64,6]{0,1:T(8,128)}, u32[]{:S(2)}) copy-start(f32[64,6]{0,1:T(8,128)} %param.13) | copy-start | bytes 4612
  246.3 45.6 %all-to-all-start.1 = ((bf16[128,6,512]{2,1,0:T(8,128)(2,1)}), bf16[128,6,512]{2,1,0:T(8,128)(2,1)}, u32[]{:S(2)}, u32[]{:S(2)}) async-start(bf16[128,6,512]{2,1,0:T(8,128)(2,1)} %reshape.73), calls=%async_computation.1 | async-start | bytes 2097152 | tf_op jit(solution)/shard_map/all_to_all | solution.py:45
  293.2 14.2 %copy-start.5 = (f32[512]{0:T(512)S(1)}, f32[512]{0:T(512)}, u32[]{:S(2)}) copy-start(f32[512]{0:T(512)} %param.17) | copy-start | bytes 6148
Sparse Core Ops, SparseCore 0:
  11.3 58.2 all-reduce.1
  203.7 38.5 all-gather.1
where the time goes:
time: 317 us; the launch traced here: 316 us
  waiting for transfers between devices  123 us (39%)
  blocking collectives  121 us (38%)
  local copies, waits for them, and re-layouts  28.7 us (9%)
  starting transfers between devices  14.7 us (5%)
  between operations  13.6 us (4%)
  matrix products  9.02 us (3%)
  other arithmetic  6.31 us (2%)
    all_to_all x1, blocking collectives, body(): lax.all_to_all(outgoing, 'req', split_axis=0, concat_axis=0, tiled=True)  111 us
    psum x1, waiting for transfers between devices, body(): projected = lax.psum(partial_value, 'tp')  53.9 us
    all_gather x1, waiting for transfers between devices, body(): lax.all_gather(hidden, 'tp', axis=1, tiled=True)  38.7 us
    all_to_all x1, waiting for transfers between devices, body(): lax.all_to_all(expert_out, 'req', split_axis=0, concat_axis=0, tiled=True)  30.2 us
    all_to_all x1, starting transfers between devices, body(): lax.all_to_all(expert_out, 'req', split_axis=0, concat_axis=0, tiled=True)  14.6 us
    psum x1, blocking collectives, body(): square_total = lax.psum(square_part, 'tp')  9.8 us
  transfers between devices with their start and end apart: 3, of which 3 were waited for; matrix products, arithmetic and copies ran while one was open for 2% of the time, Pallas kernels for 0%

commit v1 on v0

--- a/solution.py
+++ b/solution.py
@@ -37,7 +37,9 @@
     up_act = jnp.dot(expert_rows, up_local, preferred_element_type=jnp.float32)
     hidden = (jax.nn.silu(gate_act) * up_act).astype(jnp.bfloat16)
     expert_out = jnp.dot(
-        lax.all_gather(hidden, "tp", axis=1, tiled=True),
+        jnp.concatenate(
+            lax.all_to_all(jnp.stack([hidden] * lax.axis_size("tp")), "tp", 0, 0), axis=1
+        ),
         down_local,
         preferred_element_type=jnp.float32,
     )

time: 317 us -> 302 us (0.953)
  waiting for transfers between devices: 123 us -> 84.2 us
  blocking collectives: 121 us -> 143 us
  starting transfers between devices: 14.7 us -> 18.1 us
    all_gather x1 -> x0, waiting for transfers between devices: 38.7 us -> none  [body(): lax.all_gather(hidden, 'tp', axis=1, tiled=True)]
    all_to_all x0 -> x1, blocking collectives: none -> 23.2 us  [body(): lax.all_to_all(jnp.stack([hidden] * lax.axis_size('tp')), 'tp', 0, 0)]
    all_to_all x1, starting transfers between devices: 14.6 us -> 18.1 us  [body(): lax.all_to_all(expert_out, 'req', split_axis=0, concat_axis=0, tiled=True)]
  transfers between devices with their start and end apart: 3 -> 2, of which waited for: 3 -> 2; matrix products, arithmetic and copies ran while one was open for 2% -> 2% of each run, Pallas kernels for 0% -> 0%
where the time goes in v1:
time: 302 us; the launch traced here: 301 us
  blocking collectives  143 us (47%)
  waiting for transfers between devices  84.2 us (28%)
  local copies, waits for them, and re-layouts  29 us (10%)
  starting transfers between devices  18.1 us (6%)
  between operations  13.6 us (5%)
  matrix products  6.61 us (2%)
  other arithmetic  6.31 us (2%)
    all_to_all x1, blocking collectives, body(): lax.all_to_all(outgoing, 'req', split_axis=0, concat_axis=0, tiled=True)  111 us
    psum x1, waiting for transfers between devices, body(): projected = lax.psum(partial_value, 'tp')  53.9 us
    all_to_all x1, waiting for transfers between devices, body(): lax.all_to_all(expert_out, 'req', split_axis=0, concat_axis=0, tiled=True)  30.2 us
    all_to_all x1, blocking collectives, body(): lax.all_to_all(jnp.stack([hidden] * lax.axis_size('tp')), 'tp', 0, 0)  23.2 us
    all_to_all x1, starting transfers between devices, body(): lax.all_to_all(expert_out, 'req', split_axis=0, concat_axis=0, tiled=True)  18.1 us
    psum x1, blocking collectives, body(): square_total = lax.psum(square_part, 'tp')  8.9 us
    reshape x1, local copies, waits for them, and re-layouts, body(): expert_rows = incoming.reshape(slot_count * capacity, full_width)  6.34 us
    reshape x1, local copies, waits for them, and re-layouts, body(): projected.astype(jnp.bfloat16)[source_row]  6.25 us
  transfers between devices with their start and end apart: 2, of which 2 were waited for; matrix products, arithmetic and copies ran while one was open for 2% of the time, Pallas kernels for 0%

profile of v1, /device:TPU:8, one launch (start us, length us, event | category | flops | bytes accessed | tf_op | source)
XLA Modules:
  0.0 300.9 jit_solution(10026098008700047942)
XLA Ops:
  6.5 1.6 copy-done
  8.1 1.3 fusion.12
  9.4 0.9 add_dynamic-update-slice_fusion
  10.3 0.8 copy-done.2
  12.6 2.9 scatter_custom_fusion
  15.6 53.9 %all-reduce.2.cloned.1.call-done = f32[64,2048]{1,0:T(8,128)} async-done(((f32[64,2048]{1,0:T(8,128)}), f32[64,2048]{1,0:T(8,128)}) %all-reduce.2.cloned.1.call-update) | async-done | bytes 524304 | tf_op jit(solution)/shard_map/psum | solution.py:31
  69.5 1.1 convert_element_type.27
  70.6 4.3 %gather_fusion = bf16[768,2048]{1,0:T(8,128)(2,1)} fusion(bf16[64,2048]{1,0:T(8,128)(2,1)S(1)} %convert_element_type.27, s32[1024]{0:T(1024)S(1)} %pad_clamp_fusion.1), kind=kCustom, calls=%fused_computation | custom fusion | bytes 6294528 | tf_op jit(solution)/shard_map/gather | solution.py:33
  74.9 6.3 %reshape.79 = bf16[128,6,2048]{2,1,0:T(8,128)(2,1)} reshape(bf16[768,2048]{1,0:T(8,128)(2,1)} %gather_fusion) | data formatting | bytes 6291456 | tf_op jit(solution)/shard_map/reshape | solution.py:33
  81.1 111.0 %all_to_all.15 = bf16[128,6,2048]{2,1,0:T(8,128)(2,1)} all-to-all(bf16[128,6,2048]{2,1,0:T(8,128)(2,1)} %reshape.79), channel_id=1, replica_groups=mesh['req'=128,'tp'=4] {'req'}, dimensions={0} | all-to-all | bytes 6291456 | tf_op jit(solution)/shard_map/all_to_all | solution.py:34
  192.1 6.3 %reshape.80 = bf16[768,2048]{1,0:T(8,128)(2,1)} reshape(bf16[128,6,2048]{2,1,0:T(8,128)(2,1)} %all_to_all.15) | data formatting | bytes 6291456 | tf_op jit(solution)/shard_map/reshape | solution.py:35
  198.4 3.3 %fusion.3 = f32[768,256]{1,0:T(8,128)S(1)} fusion(bf16[768,2048]{1,0:T(8,128)(2,1)} %reshape.80, bf16[1,2048,256]{2,1,0:T(8,128)(2,1)} %param.14), kind=kOutput, calls=%fused_computation.8 | convolution fusion | flops 805306368 | bytes 4980736 | tf_op jit(solution)/shard_map/dot_general | solution.py:36
  201.9 1.0 fusion
  203.2 23.2 %all_to_all.16 = bf16[4,768,256]{1,2,0:T(8,128)(2,1)S(1)} all-to-all(bf16[4,768,256]{1,2,0:T(8,128)(2,1)S(1)} %stack.2), channel_id=1, replica_groups=mesh['req'=128,'tp'=4] {'tp'}, dimensions={0} | all-to-all | bytes 3145728 | tf_op jit(solution)/shard_map/all_to_all | solution.py:41
  226.4 1.0 convolution_convert_fusion
  227.4 1.3 reshape.83
  228.7 18.1 %all-to-all-start.2 = ((bf16[128,6,512]{2,1,0:T(8,128)(2,1)}), bf16[128,6,512]{2,1,0:T(8,128)(2,1)}, u32[]{:S(2)}, u32[]{:S(2)}) async-start(bf16[128,6,512]{2,1,0:T(8,128)(2,1)} %reshape.83), calls=%async_computation.2 | async-start | bytes 2097152 | tf_op jit(solution)/shard_map/all_to_all | solution.py:47
  247.5 30.2 %all-to-all-done.2 = bf16[128,6,512]{2,1,0:T(8,128)(2,1)} async-done(((bf16[128,6,512]{2,1,0:T(8,128)(2,1)}), bf16[128,6,512]{2,1,0:T(8,128)(2,1)}, u32[]{:S(2)}, u32[]{:S(2)}) %all-to-all-start.2) | async-done | bytes 786464 | tf_op jit(solution)/shard_map/all_to_all | solution.py:47
  277.8 1.4 reshape.84
  279.2 2.1 gather_fusion.1
  281.3 1.1 multiply_reduce_fusion
  282.5 1.0 multiply_reduce_fusion.1
  283.5 8.9 %psum.15 = f32[64]{0:T(128)S(1)} all-reduce(f32[64]{0:T(128)S(1)} %multiply_reduce_fusion.1), channel_id=1, replica_groups=mesh['req'=128,'tp'=4] {'tp'}, use_global_device_ids=true, to_apply=%region_7.8 | all-reduce | flops 64 | bytes 512 | tf_op jit(solution)/shard_map/psum | solution.py:53
  292.4 1.6 multiply_convert_fusion
  (40 shorter events, 2.7 us)
Async XLA Ops:
  6.5 1.6 copy-start
  6.5 4.6 %copy-start.3 = (s32[64,6]{0,1:T(8,128)S(1)}, s32[64,6]{0,1:T(8,128)}, u32[]{:S(2)}) copy-start(s32[64,6]{0,1:T(8,128)} %param.12) | copy-start | bytes 4612
  6.5 63.0 %all-reduce.2.cloned.1.call-start = ((), (), s32[]{:S(2)}) async-start(), calls=%async_computation.3 | async-start | bytes 1048576 | tf_op jit(solution)/shard_map/psum | solution.py:31
  10.3 0.8 copy-start.2
  198.4 3.3 %copy-start.1 = (bf16[768,2048]{1,0:T(8,128)(2,1)S(1)}, bf16[768,2048]{1,0:T(8,128)(2,1)}, u32[]{:S(2)}) copy-start(bf16[768,2048]{1,0:T(8,128)(2,1)} %reshape.80) | copy-start | bytes 9437188
  198.4 3.4 %copy-start.6 = (bf16[1,2048,256]{2,1,0:T(8,128)(2,1)S(1)}, bf16[1,2048,256]{2,1,0:T(8,128)(2,1)}, u32[]{:S(2)}) copy-start(bf16[1,2048,256]{2,1,0:T(8,128)(2,1)} %param.15) | copy-start | bytes 3145732
  203.0 23.3 %copy-start.7 = (bf16[1,1024,512]{2,1,0:T(8,128)(2,1)S(1)}, bf16[1,1024,512]{2,1,0:T(8,128)(2,1)}, u32[]{:S(2)}) copy-start(bf16[1,1024,512]{2,1,0:T(8,128)(2,1)} %param.16) | copy-start | bytes 3145732
  227.4 19.4 %copy-start.4 = (f32[64,6]{0,1:T(8,128)S(1)}, f32[64,6]{0,1:T(8,128)}, u32[]{:S(2)}) copy-start(f32[64,6]{0,1:T(8,128)} %param.13) | copy-start | bytes 4612
  228.7 49.1 %all-to-all-start.2 = ((bf16[128,6,512]{2,1,0:T(8,128)(2,1)}), bf16[128,6,512]{2,1,0:T(8,128)(2,1)}, u32[]{:S(2)}, u32[]{:S(2)}) async-start(bf16[128,6,512]{2,1,0:T(8,128)(2,1)} %reshape.83), calls=%async_computation.2 | async-start | bytes 2097152 | tf_op jit(solution)/shard_map/all_to_all | solution.py:47
  279.1 13.3 %copy-start.5 = (f32[512]{0:T(512)S(1)}, f32[512]{0:T(512)}, u32[]{:S(2)}) copy-start(f32[512]{0:T(512)} %param.17) | copy-start | bytes 6148
Sparse Core Ops, SparseCore 0:
  11.3 58.2 all-reduce.1

commit v2 on v0

--- a/solution.py
+++ b/solution.py
@@ -48,7 +48,7 @@
     routed_sum = jnp.sum(picked * gates[:, :, None], axis=1)
     combined = own_part + routed_sum
     square_part = jnp.sum(combined * combined, axis=1)
-    square_total = lax.psum(square_part, "tp")
+    square_total = jnp.sum(lax.all_gather(square_part, "tp"), axis=0)
     scale = lax.rsqrt(square_total / full_width + 1e-06)
     return (combined * scale[:, None] * norm_gain[None, :]).astype(jnp.bfloat16)
 

time: 317 us -> 317 us (level)
    psum x1 -> x0, blocking collectives: 9.8 us -> none  [body(): square_total = lax.psum(square_part, 'tp')]
    unnamed x0 -> x1, blocking collectives: none -> 9.77 us
where the time goes in v2:
time: 317 us; the launch traced here: 316 us
  waiting for transfers between devices  121 us (38%)
  blocking collectives  121 us (38%)
  local copies, waits for them, and re-layouts  30.3 us (10%)
  starting transfers between devices  14.7 us (5%)
  between operations  14.3 us (5%)
  matrix products  9.02 us (3%)
  other arithmetic  6.34 us (2%)
    all_to_all x1, blocking collectives, body(): lax.all_to_all(outgoing, 'req', split_axis=0, concat_axis=0, tiled=True)  111 us
    psum x1, waiting for transfers between devices, body(): projected = lax.psum(partial_value, 'tp')  53.9 us
    all_gather x1, waiting for transfers between devices, body(): lax.all_gather(hidden, 'tp', axis=1, tiled=True)  38.7 us
    all_to_all x1, waiting for transfers between devices, body(): lax.all_to_all(expert_out, 'req', split_axis=0, concat_axis=0, tiled=True)  28.3 us
    all_to_all x1, starting transfers between devices, body(): lax.all_to_all(expert_out, 'req', split_axis=0, concat_axis=0, tiled=True)  14.6 us
    unnamed x1, blocking collectives  9.77 us
  transfers between devices with their start and end apart: 3, of which 3 were waited for; matrix products, arithmetic and copies ran while one was open for 2% of the time, Pallas kernels for 0%

profile of v2, /device:TPU:8, one launch (start us, length us, event | category | flops | bytes accessed | tf_op | source)
XLA Modules:
  0.0 316.2 jit_solution(17207909610854124284)
XLA Ops:
  6.5 1.6 copy-done
  8.1 1.3 fusion.12
  9.4 0.9 add_dynamic-update-slice_fusion
  12.7 2.9 scatter_custom_fusion
  15.6 53.9 %all-reduce.3.cloned.1.call-done = f32[64,2048]{1,0:T(8,128)} async-done(((f32[64,2048]{1,0:T(8,128)}), f32[64,2048]{1,0:T(8,128)}) %all-reduce.3.cloned.1.call-update) | async-done | bytes 524304 | tf_op jit(solution)/shard_map/psum | solution.py:31
  69.5 1.1 convert_element_type.27
  70.6 4.3 %gather_fusion = bf16[768,2048]{1,0:T(8,128)(2,1)} fusion(bf16[64,2048]{1,0:T(8,128)(2,1)S(1)} %convert_element_type.27, s32[1024]{0:T(1024)S(1)} %pad_clamp_fusion.1), kind=kCustom, calls=%fused_computation | custom fusion | bytes 6294528 | tf_op jit(solution)/shard_map/gather | solution.py:33
  74.9 6.3 %reshape.75 = bf16[128,6,2048]{2,1,0:T(8,128)(2,1)} reshape(bf16[768,2048]{1,0:T(8,128)(2,1)} %gather_fusion) | data formatting | bytes 6291456 | tf_op jit(solution)/shard_map/reshape | solution.py:33
  81.1 111.0 %all_to_all.10 = bf16[128,6,2048]{2,1,0:T(8,128)(2,1)} all-to-all(bf16[128,6,2048]{2,1,0:T(8,128)(2,1)} %reshape.75), channel_id=1, replica_groups=mesh['req'=128,'tp'=4] {'req'}, dimensions={0} | all-to-all | bytes 6291456 | tf_op jit(solution)/shard_map/all_to_all | solution.py:34
  192.1 6.3 %reshape.76 = bf16[768,2048]{1,0:T(8,128)(2,1)} reshape(bf16[128,6,2048]{2,1,0:T(8,128)(2,1)} %all_to_all.10) | data formatting | bytes 6291456 | tf_op jit(solution)/shard_map/reshape | solution.py:35
  198.4 3.3 %fusion.3 = f32[768,256]{1,0:T(8,128)S(1)} fusion(bf16[768,2048]{1,0:T(8,128)(2,1)} %reshape.76, bf16[1,2048,256]{2,1,0:T(8,128)(2,1)} %param.14), kind=kOutput, calls=%fused_computation.8 | convolution fusion | flops 805306368 | bytes 4980736 | tf_op jit(solution)/shard_map/dot_general | solution.py:36
  201.9 1.7 fusion
  203.6 38.7 %all-gather.3.cloned.1.call-done = bf16[768,1024]{1,0:T(8,128)(2,1)} async-done(((bf16[768,256]{1,0:T(8,128)(2,1)}), bf16[768,1024]{1,0:T(8,128)(2,1)}) %all-gather.3.cloned.1.call-update) | async-done | bytes 1572880 | tf_op jit(solution)/shard_map/all_gather | solution.py:40
  242.3 2.7 convolution_convert_fusion
  245.0 1.3 reshape.77
  246.3 14.6 %all-to-all-start.1 = ((bf16[128,6,512]{2,1,0:T(8,128)(2,1)}), bf16[128,6,512]{2,1,0:T(8,128)(2,1)}, u32[]{:S(2)}, u32[]{:S(2)}) async-start(bf16[128,6,512]{2,1,0:T(8,128)(2,1)} %reshape.77), calls=%async_computation.1 | async-start | bytes 2097152 | tf_op jit(solution)/shard_map/all_to_all | solution.py:45
  261.6 1.3 dynamic-slice
  263.5 28.3 %all-to-all-done.1 = bf16[128,6,512]{2,1,0:T(8,128)(2,1)} async-done(((bf16[128,6,512]{2,1,0:T(8,128)(2,1)}), bf16[128,6,512]{2,1,0:T(8,128)(2,1)}, u32[]{:S(2)}, u32[]{:S(2)}) %all-to-all-start.1) | async-done | bytes 786464 | tf_op jit(solution)/shard_map/all_to_all | solution.py:45
  291.9 1.4 reshape.78
  293.3 2.1 gather_fusion.1
  295.4 1.1 multiply_reduce_fusion
  296.6 1.0 multiply_reduce_fusion.1
  297.9 9.8 %all-reduce = f32[256]{0:T(256)S(1)} all-reduce(f32[256]{0:T(256)S(1)} %dynamic-update-slice), channel_id=2, replica_groups=mesh['req'=128,'tp'=4] {'tp'}, use_global_device_ids=true, to_apply=%add | all-reduce | flops 256 | bytes 2048
  307.8 1.6 multiply_convert_fusion
  (43 shorter events, 3.6 us)
Async XLA Ops:
  6.5 1.6 copy-start
  6.5 4.6 %copy-start.3 = (s32[64,6]{0,1:T(8,128)S(1)}, s32[64,6]{0,1:T(8,128)}, u32[]{:S(2)}) copy-start(s32[64,6]{0,1:T(8,128)} %param.12) | copy-start | bytes 4612
  6.5 63.0 %all-reduce.3.cloned.1.call-start = ((), (), s32[]{:S(2)}) async-start(), calls=%async_computation.2 | async-start | bytes 1048576 | tf_op jit(solution)/shard_map/psum | solution.py:31
  10.3 0.8 copy-start.2
  11.1 231.1 %all-gather.3.cloned.1.call-start = ((), (), s32[]{:S(2)}) async-start(), calls=%async_computation.3 | async-start | bytes 1966080 | tf_op jit(solution)/shard_map/all_gather | solution.py:40
  198.4 3.3 %copy-start.1 = (bf16[768,2048]{1,0:T(8,128)(2,1)S(1)}, bf16[768,2048]{1,0:T(8,128)(2,1)}, u32[]{:S(2)}) copy-start(bf16[768,2048]{1,0:T(8,128)(2,1)} %reshape.76) | copy-start | bytes 9437188
  198.4 3.4 %copy-start.6 = (bf16[1,2048,256]{2,1,0:T(8,128)(2,1)S(1)}, bf16[1,2048,256]{2,1,0:T(8,128)(2,1)}, u32[]{:S(2)}) copy-start(bf16[1,2048,256]{2,1,0:T(8,128)(2,1)} %param.15) | copy-start | bytes 3145732
  245.0 15.9 %copy-start.4 = (f32[64,6]{0,1:T(8,128)S(1)}, f32[64,6]{0,1:T(8,128)}, u32[]{:S(2)}) copy-start(f32[64,6]{0,1:T(8,128)} %param.13) | copy-start | bytes 4612
  246.3 45.6 %all-to-all-start.1 = ((bf16[128,6,512]{2,1,0:T(8,128)(2,1)}), bf16[128,6,512]{2,1,0:T(8,128)(2,1)}, u32[]{:S(2)}, u32[]{:S(2)}) async-start(bf16[128,6,512]{2,1,0:T(8,128)(2,1)} %reshape.77), calls=%async_computation.1 | async-start | bytes 2097152 | tf_op jit(solution)/shard_map/all_to_all | solution.py:45
  293.2 14.5 %copy-start.5 = (f32[512]{0:T(512)S(1)}, f32[512]{0:T(512)}, u32[]{:S(2)}) copy-start(f32[512]{0:T(512)} %param.17) | copy-start | bytes 6148
Sparse Core Ops, SparseCore 0:
  11.3 58.2 all-reduce.2
  203.7 38.5 all-gather.2
